TPU v7x, 32 devices: a whole 2x2x4 slice. The times are simulated.
32 devices in a mesh: groups: 2 (over x), spatial: 16 (over z, y, core).
Axes of the slice: x: 2, y: 2, z: 4, core: 2. Of those that a mesh axis runs over, the one named last changes fastest.
Arguments:
- fields: bfloat16 [1024, 128, 768], P(('groups', 'spatial')), parts along dimension 0, may hold values from -6 to 6
- norm1_gain: float32 [768], replicated, may hold values from 0.5 to 1.5
- norm1_bias: float32 [768], replicated, may hold values from -3 to 3
- spectral_w1: float32 [2, 8, 96, 96], replicated, may hold values from -0.4375 to 0.4375
- spectral_b1: float32 [2, 8, 96], replicated, may hold values from -3 to 3
- spectral_w2: float32 [2, 8, 96, 96], replicated, may hold values from -0.4375 to 0.4375
- spectral_b2: float32 [2, 8, 96], replicated, may hold values from -3 to 3
- norm2_gain: float32 [768], replicated, may hold values from 0.5 to 1.5
- norm2_bias: float32 [768], replicated, may hold values from -3 to 3
- fc1_weight: bfloat16 [768, 3072], replicated, may hold values from -0.21875 to 0.21875
- fc1_bias: float32 [3072], replicated, may hold values from -3 to 3
- fc2_weight: bfloat16 [3072, 768], replicated, may hold values from -0.109375 to 0.109375
- fc2_bias: float32 [768], replicated, may hold values from -3 to 3
Outputs:
- next_state: bfloat16 [1024, 128, 768], P(('groups', 'spatial')), parts along dimension 0
- anomaly: bfloat16 [1024, 128, 768], P(('groups', 'spatial')), parts along dimension 0
There are 2 independent parts, one for each index of `groups`. A program takes and returns all parts, laid end to end along the dimension named above; an argument that names none is the same for every part. Nothing has to cross between parts.
All inputs are finite; a program needn't handle non-finite values.
Results may differ from a plain program's by a relative error of at most 0.0056.
Values may be sent and summed in bfloat16 or wider, within the bound.
A program may use at most 192 MiB of HBM per device.

v0:
```python
import math
import jax
import jax.numpy as jnp
from jax import lax
from jax.sharding import Mesh, PartitionSpec as P

MEMBERS = 8
EPSILON = 1e-06
SHRINK = 0.01
FULL_PRECISION = lax.Precision.HIGHEST


def from_behind(block, axis, distance):
    devices = range(lax.axis_size(axis))
    route = [((i - distance) % len(devices), i) for i in devices]
    return lax.ppermute(block, axis, route)


def layer_norm(values, gain, offset_term):
    center = values - jnp.mean(values, axis=-1, keepdims=True)
    spread = jnp.mean(center * center, axis=-1, keepdims=True)
    return center * lax.rsqrt(spread + EPSILON) * gain + offset_term


def soft_shrink(values):
    return jnp.where(
        values > SHRINK, values - SHRINK, jnp.where(values < -SHRINK, values + SHRINK, 0.0)
    )


def contract(form, left, right):
    return jnp.einsum(form, left, right, precision=FULL_PRECISION)


def block_product(values, weight):
    return jnp.einsum("...bi,bio->...bo", values, weight, precision=FULL_PRECISION)


def angle_table(first_len, second_len, modulus):
    first_index = lax.broadcasted_iota(jnp.int32, (first_len, second_len), 0)
    second_index = lax.broadcasted_iota(jnp.int32, (first_len, second_len), 1)
    phase = first_index * second_index % modulus
    return phase.astype(jnp.float32) * (2.0 * math.pi / modulus)


def spectral_layer(real_part, imag_part, w_first, b_first, w_second, b_second):
    shape = real_part.shape
    block_count = w_first.shape[1]
    split_shape = shape[:-1] + (block_count, shape[-1] // block_count)
    real_part = real_part.reshape(split_shape)
    imag_part = imag_part.reshape(split_shape)
    hidden_real = jax.nn.relu(
        block_product(real_part, w_first[0]) - block_product(imag_part, w_first[1]) + b_first[0]
    )
    hidden_imag = jax.nn.relu(
        block_product(imag_part, w_first[0]) + block_product(real_part, w_first[1]) + b_first[1]
    )
    mixed_real = (
        block_product(hidden_real, w_second[0])
        - block_product(hidden_imag, w_second[1])
        + b_second[0]
    )
    mixed_imag = (
        block_product(hidden_imag, w_second[0])
        + block_product(hidden_real, w_second[1])
        + b_second[1]
    )
    return (soft_shrink(mixed_real).reshape(shape), soft_shrink(mixed_imag).reshape(shape))


def longitude_forward(normed, lon_len):
    angles = angle_table(lon_len, lon_len // 2, lon_len)
    factor = 1.0 / math.sqrt(lon_len)
    real_part = contract("rld,lk->rkd", normed, jnp.cos(angles) * factor)
    imag_part = -contract("rld,lk->rkd", normed, jnp.sin(angles) * factor)
    return (real_part, imag_part)


def longitude_inverse(real_part, imag_part, lon_len):
    half_len = lon_len // 2
    angles = angle_table(lon_len, half_len, lon_len)
    column_index = lax.broadcasted_iota(jnp.int32, (1, half_len), 1)
    weights = jnp.where(column_index == 0, 1.0, 2.0) / math.sqrt(lon_len)
    cosine_table = jnp.cos(angles) * weights
    sine_table = jnp.sin(angles) * weights
    return contract("rkd,lk->rld", real_part, cosine_table) - contract(
        "rkd,lk->rld", imag_part, sine_table
    )


def latitude_work(real_part, imag_part, w_first, b_first, w_second, b_second):
    member_rows, mode_count, channels = real_part.shape
    lat_len = member_rows // MEMBERS
    angles = angle_table(lat_len, lat_len, lat_len)
    factor = 1.0 / math.sqrt(lat_len)
    cosine_table = jnp.cos(angles) * factor
    sine_table = jnp.sin(angles) * factor
    grid_real = real_part.reshape(MEMBERS, lat_len, mode_count, channels)
    grid_imag = imag_part.reshape(MEMBERS, lat_len, mode_count, channels)
    spec_real = contract("qp,mpkd->mqkd", cosine_table, grid_real) + contract(
        "qp,mpkd->mqkd", sine_table, grid_imag
    )
    spec_imag = contract("qp,mpkd->mqkd", cosine_table, grid_imag) - contract(
        "qp,mpkd->mqkd", sine_table, grid_real
    )
    mixed_real, mixed_imag = spectral_layer(
        spec_real, spec_imag, w_first, b_first, w_second, b_second
    )
    back_real = contract("qp,mpkd->mqkd", cosine_table, mixed_real) - contract(
        "qp,mpkd->mqkd", sine_table, mixed_imag
    )
    back_imag = contract("qp,mpkd->mqkd", cosine_table, mixed_imag) + contract(
        "qp,mpkd->mqkd", sine_table, mixed_real
    )
    return (
        back_real.reshape(member_rows, mode_count, channels),
        back_imag.reshape(member_rows, mode_count, channels),
    )


def on_device(
    fields,
    norm1_gain,
    norm1_bias,
    spectral_w1,
    spectral_b1,
    spectral_w2,
    spectral_b2,
    norm2_gain,
    norm2_bias,
    fc1_weight,
    fc1_bias,
    fc2_weight,
    fc2_bias,
):
    row_count, lon_len, channels = fields.shape
    state = fields.astype(jnp.float32)
    normed = layer_norm(state, norm1_gain, norm1_bias)
    real_part, imag_part = longitude_forward(normed, lon_len)
    real_part, imag_part = (
        lax.all_to_all(real_part, "spatial", split_axis=1, concat_axis=0, tiled=True),
        lax.all_to_all(imag_part, "spatial", split_axis=1, concat_axis=0, tiled=True),
    )
    real_part, imag_part = latitude_work(
        real_part, imag_part, spectral_w1, spectral_b1, spectral_w2, spectral_b2
    )
    real_part, imag_part = (
        lax.all_to_all(real_part, "spatial", split_axis=0, concat_axis=1, tiled=True),
        lax.all_to_all(imag_part, "spatial", split_axis=0, concat_axis=1, tiled=True),
    )
    filtered = longitude_inverse(real_part, imag_part, lon_len)
    residual = (filtered + normed + state).reshape(row_count * lon_len, channels)
    normed2 = layer_norm(residual, norm2_gain, norm2_bias).astype(jnp.bfloat16)
    hidden = jax.nn.gelu(
        jnp.dot(normed2, fc1_weight, preferred_element_type=jnp.float32) + fc1_bias,
        approximate=False,
    ).astype(jnp.bfloat16)
    updated = residual + jnp.dot(hidden, fc2_weight, preferred_element_type=jnp.float32) + fc2_bias
    next_state = updated.astype(jnp.bfloat16).reshape(row_count, lon_len, channels)
    return next_state


def ensemble_step(next_state):
    state_values = next_state.astype(jnp.float32)
    summed = lax.psum(state_values, "member")
    anomaly = (state_values - summed / MEMBERS).astype(jnp.bfloat16)
    return (next_state, anomaly)


def solution(mesh):
    placed = (
        P(("groups", "spatial"), None, None),
        P(),
        P(),
        P(),
        P(),
        P(),
        P(),
        P(),
        P(),
        P(),
        P(),
        P(),
        P(),
    )
    update = jax.shard_map(
        on_device,
        mesh=mesh,
        in_specs=placed,
        out_specs=P(("groups", "spatial"), None, None),
        check_vma=False,
    )
    member_span = mesh.shape["spatial"] // MEMBERS
    ensemble_mesh = Mesh(
        mesh.devices.reshape(mesh.shape["groups"], MEMBERS, member_span),
        ("groups", "member", "half"),
    )
    member_rows = P(("groups", "member", "half"), None, None)
    spread = jax.shard_map(
        ensemble_step,
        mesh=ensemble_mesh,
        in_specs=(member_rows,),
        out_specs=(member_rows, member_rows),
        check_vma=False,
    )

    def step(*args):
        return spread(update(*args))

    return step
```

profile of v0, /device:TPU:0, one launch (start us, length us, event | category | flops | bytes accessed | tf_op | source)
XLA Modules:
  0.0 1506.0 jit_solution(8603126026089970054)
XLA Ops:
  31.3 12.0 fusion.94
  49.6 95.7 %all-to-all-done.1 = f32[32,64,768]{2,0,1:T(8,128)} async-done(((f32[32,64,768]{2,0,1:T(8,128)}), f32[32,64,768]{2,0,1:T(8,128)}, u32[]{:S(2)}, u32[]{:S(2)}) %all-to-all-start.1) | async-done | bytes 6291488 | tf_op jit(solution)/shard_map/all_to_all | solution.py:142
  145.3 28.5 %all-to-all-start = ((f32[32,64,768]{2,0,1:T(8,128)}), f32[32,64,768]{2,0,1:T(8,128)}, u32[]{:S(2)}, u32[]{:S(2)}) async-start(f32[32,64,768]{2,0,1:T(8,128)} %copy.57), calls=%async_computation | async-start | bytes 12582912 | tf_op jit(solution)/shard_map/all_to_all | solution.py:141
  193.1 94.8 %all-to-all-done = f32[32,64,768]{2,0,1:T(8,128)} async-done(((f32[32,64,768]{2,0,1:T(8,128)}), f32[32,64,768]{2,0,1:T(8,128)}, u32[]{:S(2)}, u32[]{:S(2)}) %all-to-all-start) | async-done | bytes 6291488 | tf_op jit(solution)/shard_map/all_to_all | solution.py:141
  302.2 9.9 reshape.102
  312.1 13.7 fusion.58
  325.9 9.9 fusion.60
  343.9 9.9 reshape.101
  353.8 13.1 add_maximum_fusion
  376.5 9.9 fusion.52
  396.0 14.9 select_bitcast_fusion
  410.9 10.9 copy.70
  431.5 12.2 select_bitcast_fusion.1
  443.7 10.9 copy.69
  488.4 28.2 %all-to-all-start.2 = ((f32[512,4,768]{2,1,0:T(4,128)}), f32[512,4,768]{2,1,0:T(4,128)}, u32[]{:S(2)}, u32[]{:S(2)}) async-start(f32[512,4,768]{2,1,0:T(4,128)} %copy.72), calls=%async_computation.2 | async-start | bytes 12582912 | tf_op jit(solution)/shard_map/all_to_all | solution.py:148
  539.2 91.6 %all-to-all-done.2 = f32[512,4,768]{2,1,0:T(4,128)} async-done(((f32[512,4,768]{2,1,0:T(4,128)}), f32[512,4,768]{2,1,0:T(4,128)}, u32[]{:S(2)}, u32[]{:S(2)}) %all-to-all-start.2) | async-done | bytes 6291488 | tf_op jit(solution)/shard_map/all_to_all | solution.py:148
  630.7 28.5 %all-to-all-start.3 = ((f32[512,4,768]{2,1,0:T(4,128)}), f32[512,4,768]{2,1,0:T(4,128)}, u32[]{:S(2)}, u32[]{:S(2)}) async-start(f32[512,4,768]{2,1,0:T(4,128)} %copy.76), calls=%async_computation.3 | async-start | bytes 12582912 | tf_op jit(solution)/shard_map/all_to_all | solution.py:149
  677.7 95.6 %all-to-all-done.3 = f32[512,4,768]{2,1,0:T(4,128)} async-done(((f32[512,4,768]{2,1,0:T(4,128)}), f32[512,4,768]{2,1,0:T(4,128)}, u32[]{:S(2)}, u32[]{:S(2)}) %all-to-all-start.3) | async-done | bytes 6291488 | tf_op jit(solution)/shard_map/all_to_all | solution.py:149
  792.0 15.1 %fusion.134 = f32[128,32,768]{2,0,1:T(8,128)} fusion(f32[32,64,768]{2,1,0:T(8,128)} %all_to_all.57, f32[64]{0:T(128)S(1)} %fusion.172), kind=kOutput, calls=%fused_computation.149 | convolution fusion | flops 2416041984 | bytes 18874624 | tf_op jit(solution)/shard_map/rkd,lk->rld/dot_general | solution.py:32
  807.1 19.1 %fusion.262 = (f32[32,128]{1,0:T(8,128)S(1)}, f32[32,128,768]{2,1,0:T(8,128)S(1)}) fusion(f32[768]{0:T(1024)S(1)} %copy-done.16, f32[768]{0:T(1024)S(1)} %copy-done.18, f32[32,128]{1,0:T(8,128)S(1)} %copy-done.12, f32[32,128]{1,0:T(8,128)S(1)} %copy-done.10, bf16[32,128,768]{2,1,0:T(8,128)(2,1)} %param.14, f32[128,32,768]{2,0,1:T(8,128)} %fusion.134, ...), kind=kOutput, calls=%fused_computation.276 | convolution fusion | flops 2444349440 | bytes 37804288 | tf_op jit(solution)/shard_map/rkd,lk->rld/dot_general | solution.py:32
  830.8 126.3 %fusion.2.clone.6 = bf16[4096,3072]{1,0:T(8,128)(2,1)} fusion(bf16[4096,768]{1,0:T(8,128)(2,1)S(1)} %fusion.47, bf16[768,3072]{1,0:T(8,128)(2,1)} %param.23, f32[3072]{0:T(1024)S(1)} %copy-done.21), kind=kOutput, calls=%fused_computation.3.clone.clone.clone.clone.clone.1 | convolution fusion | flops 20157825024 | bytes 36188160 | tf_op jit(solution)/shard_map/dot_general | solution.py:155
  957.2 27.6 %fusion.49 = bf16[4096,768]{1,0:T(8,128)(2,1)} fusion(f32[32,128,768]{2,1,0:T(8,128)} %copy-done, bf16[3072,768]{1,0:T(8,128)(2,1)} %param.25, f32[768]{0:T(1024)S(1)} %copy-done.22, bf16[4096,3072]{1,0:T(8,128)(2,1)} %fusion.2.clone.6), kind=kOutput, calls=%fused_computation.61 | convolution fusion | flops 19336790016 | bytes 48761856 | tf_op jit(solution)/shard_map/dot_general | solution.py:158
  984.7 509.6 %all-reduce.1 = f32[32,128,768]{2,1,0:T(8,128)} all-reduce(bf16[32,128,768]{2,1,0:T(8,128)(2,1)} %bitcast.202), channel_id=1, replica_groups=mesh['groups'=2,'member'=8,'half'=2] {'member'}, use_global_device_ids=true, to_apply=%region_4.6 | all-reduce | flops 3145728 | bytes 18874368 | tf_op jit(solution)/shard_map/psum | solution.py:165
  1494.3 11.2 subtract_convert_fusion
  (115 shorter events, 205.0 us)
Async XLA Ops:
  5.2 26.0 %copy-start.9 = (f32[32,128]{1,0:T(8,128)}, f32[32,128]{1,0:T(8,128)S(1)}, u32[]{:S(2)}) copy-start(f32[32,128]{1,0:T(8,128)S(1)} %broadcast_multiply_fusion.1) | copy-start | bytes 49156
  7.6 23.6 %copy-start.11 = (f32[32,128]{1,0:T(8,128)}, f32[32,128]{1,0:T(8,128)S(1)}, u32[]{:S(2)}) copy-start(f32[32,128]{1,0:T(8,128)S(1)} %add_rsqrt_fusion) | copy-start | bytes 49156
  23.8 121.5 %all-to-all-start.1 = ((f32[32,64,768]{2,0,1:T(8,128)}), f32[32,64,768]{2,0,1:T(8,128)}, u32[]{:S(2)}, u32[]{:S(2)}) async-start(f32[32,64,768]{2,0,1:T(8,128)} %copy.60), calls=%async_computation.1 | async-start | bytes 12582912 | tf_op jit(solution)/shard_map/all_to_all | solution.py:142
  49.6 124.2 %copy-start.13 = (f32[2,8,96]{2,1,0:T(8,128)S(1)}, f32[2,8,96]{2,1,0:T(8,128)}, u32[]{:S(2)}) copy-start(f32[2,8,96]{2,1,0:T(8,128)} %param.18) | copy-start | bytes 18436
  49.6 124.3 %copy-start.14 = (f32[2,8,96]{2,1,0:T(8,128)S(1)}, f32[2,8,96]{2,1,0:T(8,128)}, u32[]{:S(2)}) copy-start(f32[2,8,96]{2,1,0:T(8,128)} %param.20) | copy-start | bytes 18436
  145.3 142.6 %all-to-all-start = ((f32[32,64,768]{2,0,1:T(8,128)}), f32[32,64,768]{2,0,1:T(8,128)}, u32[]{:S(2)}, u32[]{:S(2)}) async-start(f32[32,64,768]{2,0,1:T(8,128)} %copy.57), calls=%async_computation | async-start | bytes 12582912 | tf_op jit(solution)/shard_map/all_to_all | solution.py:141
  193.1 101.2 %slice-start.10 = ((s8[6291456]{0:T(1024)(128)(4,1)}), s8[2097152]{0:T(1024)(128)(4,1)S(1)}, s32[]{:S(2)}) async-start(s8[6291456]{0:T(1024)(128)(4,1)} %bitcast.200), calls=%async_computation.14 | async-start | bytes 4194304
  302.2 9.9 copy-start.5
  312.1 13.8 copy-start.1
  312.1 23.6 %slice-start.4 = ((s8[6291456]{0:T(1024)(128)(4,1)}), s8[4194304]{0:T(1024)(128)(4,1)S(1)}, s32[]{:S(2)}) async-start(s8[6291456]{0:T(1024)(128)(4,1)} %bitcast.189), calls=%async_computation.8 | async-start | bytes 8388608
  312.1 23.6 %slice-start.8 = ((s8[6291456]{0:T(1024)(128)(4,1)}), s8[4194304]{0:T(1024)(128)(4,1)S(1)}, s32[]{:S(2)}) async-start(s8[6291456]{0:T(1024)(128)(4,1)} %bitcast.198), calls=%async_computation.12 | async-start | bytes 8388608
  353.8 13.2 copy-start.6
  367.0 19.4 %slice-start = ((s8[8388608]{0:T(1024)(128)(4,1)}), s8[4194304]{0:T(1024)(128)(4,1)S(1)}, s32[]{:S(2)}) async-start(s8[8388608]{0:T(1024)(128)(4,1)} %bitcast.182), calls=%async_computation.4 | async-start | bytes 8388608
  367.0 19.4 %slice-start.6 = ((s8[8388608]{0:T(1024)(128)(4,1)}), s8[4194304]{0:T(1024)(128)(4,1)S(1)}, s32[]{:S(2)}) async-start(s8[8388608]{0:T(1024)(128)(4,1)} %bitcast.192), calls=%async_computation.10 | async-start | bytes 8388608
  376.5 9.9 slice-start.7
  396.0 14.9 copy-start.2
  488.4 36.9 %slice-start.2 = ((s8[6291456]{0:T(1024)(128)(4,1)}), s8[2097152]{0:T(1024)(128)(4,1)S(1)}, s32[]{:S(2)}) async-start(s8[6291456]{0:T(1024)(128)(4,1)} %bitcast.184), calls=%async_computation.6 | async-start | bytes 4194304
  488.4 142.3 %all-to-all-start.2 = ((f32[512,4,768]{2,1,0:T(4,128)}), f32[512,4,768]{2,1,0:T(4,128)}, u32[]{:S(2)}, u32[]{:S(2)}) async-start(f32[512,4,768]{2,1,0:T(4,128)} %copy.72), calls=%async_computation.2 | async-start | bytes 12582912 | tf_op jit(solution)/shard_map/all_to_all | solution.py:148
  630.7 142.6 %all-to-all-start.3 = ((f32[512,4,768]{2,1,0:T(4,128)}), f32[512,4,768]{2,1,0:T(4,128)}, u32[]{:S(2)}, u32[]{:S(2)}) async-start(f32[512,4,768]{2,1,0:T(4,128)} %copy.76), calls=%async_computation.3 | async-start | bytes 12582912 | tf_op jit(solution)/shard_map/all_to_all | solution.py:149
  791.9 15.1 %copy-start.10 = (f32[32,128]{1,0:T(8,128)S(1)}, f32[32,128]{1,0:T(8,128)}, u32[]{:S(2)}) copy-start(f32[32,128]{1,0:T(8,128)} %copy-done.9) | copy-start | bytes 49156
  792.0 15.1 %copy-start.12 = (f32[32,128]{1,0:T(8,128)S(1)}, f32[32,128]{1,0:T(8,128)}, u32[]{:S(2)}) copy-start(f32[32,128]{1,0:T(8,128)} %copy-done.11) | copy-start | bytes 49156
  792.0 15.1 %copy-start.16 = (f32[768]{0:T(1024)S(1)}, f32[768]{0:T(1024)}, u32[]{:S(2)}) copy-start(f32[768]{0:T(1024)} %param.16) | copy-start | bytes 9220
  792.0 15.1 %copy-start.18 = (f32[768]{0:T(1024)S(1)}, f32[768]{0:T(1024)}, u32[]{:S(2)}) copy-start(f32[768]{0:T(1024)} %param.15) | copy-start | bytes 9220
  830.8 126.3 %copy-start.22 = (f32[768]{0:T(1024)S(1)}, f32[768]{0:T(1024)}, u32[]{:S(2)}) copy-start(f32[768]{0:T(1024)} %param.26) | copy-start | bytes 9220
  (15 other events, 95.8 us)
where the time goes:
time: 1520 us; the launch traced here: 1510 us
  blocking collectives  510 us (34%)
  waiting for transfers between devices  378 us (25%)
  matrix products  367 us (24%)
  local copies, waits for them, and re-layouts  136 us (9%)
  starting transfers between devices  92.8 us (6%)
  other arithmetic  21.4 us (1%)
    psum x1, blocking collectives, ensemble_step(): summed = lax.psum(state_values, 'member')  510 us
    dot_general x1, matrix products, on_device(): jnp.dot(normed2, fc1_weight, preferred_element_type=jnp.float32) + fc1_bias  126 us
    dot_general x12, matrix products, contract(): return jnp.einsum(form, left, right, precision=FULL_PRECISION)  120 us
    all_to_all x1, waiting for transfers between devices, on_device(): lax.all_to_all(imag_part, 'spatial', split_axis=1, concat_axis=0, tiled=T...  95.7 us
    all_to_all x1, waiting for transfers between devices, on_device(): lax.all_to_all(imag_part, 'spatial', split_axis=0, concat_axis=1, tiled=T...  95.6 us
    all_to_all x1, waiting for transfers between devices, on_device(): lax.all_to_all(real_part, 'spatial', split_axis=1, concat_axis=0, tiled=T...  94.8 us
    dot_general x8, matrix products, block_product(): jnp.einsum('...bi,bio->...bo', values, weight, precision=FULL_PRECISION)  92.8 us
    all_to_all x1, waiting for transfers between devices, on_device(): lax.all_to_all(real_part, 'spatial', split_axis=0, concat_axis=1, tiled=T...  91.6 us
  transfers between devices with their start and end apart: 4, of which 4 were waited for; matrix products, arithmetic and copies ran while one was open for 5% of the time, Pallas kernels for 0%

commit v1 on v0

--- a/solution.py
+++ b/solution.py
@@ -162,7 +162,7 @@
 
 def ensemble_step(next_state):
     state_values = next_state.astype(jnp.float32)
-    summed = lax.psum(state_values, "member")
+    summed = jax.lax.all_gather(state_values, "member").sum(axis=0)
     anomaly = (state_values - summed / MEMBERS).astype(jnp.bfloat16)
     return (next_state, anomaly)
 

time: 1520 us -> 2980 us (1.96)
  waiting for transfers between devices: 378 us -> 2300 us
  blocking collectives: 510 us -> 0 us
  other arithmetic: 21.4 us -> 63.5 us
    all_gather x0 -> x1, waiting for transfers between devices: none -> 1920 us  [ensemble_step(): summed = jax.lax.all_gather(state_values, 'member').sum(axis=0)]
    psum x1 -> x0, blocking collectives: 510 us -> none  [ensemble_step(): summed = lax.psum(state_values, 'member')]
    reduce_sum x0 -> x1, other arithmetic: none -> 36 us  [ensemble_step(): summed = jax.lax.all_gather(state_values, 'member').sum(axis=0)]
  transfers between devices with their start and end apart: 4 -> 5, of which waited for: 4 -> 5; matrix products, arithmetic and copies ran while one was open for 5% -> 2% of each run, Pallas kernels for 0% -> 0%
where the time goes in v1:
time: 2980 us; the launch traced here: 2970 us
  waiting for transfers between devices  2300 us (77%)
  matrix products  366 us (12%)
  local copies, waits for them, and re-layouts  139 us (5%)
  starting transfers between devices  92.8 us (3%)
  other arithmetic  63.5 us (2%)
    all_gather x1, waiting for transfers between devices, ensemble_step(): summed = jax.lax.all_gather(state_values, 'member').sum(axis=0)  1920 us
    dot_general x1, matrix products, on_device(): jnp.dot(normed2, fc1_weight, preferred_element_type=jnp.float32) + fc1_bias  126 us
    dot_general x12, matrix products, contract(): return jnp.einsum(form, left, right, precision=FULL_PRECISION)  120 us
    all_to_all x1, waiting for transfers between devices, on_device(): lax.all_to_all(imag_part, 'spatial', split_axis=1, concat_axis=0, tiled=T...  95.7 us
    all_to_all x1, waiting for transfers between devices, on_device(): lax.all_to_all(imag_part, 'spatial', split_axis=0, concat_axis=1, tiled=T...  95.2 us
    all_to_all x1, waiting for transfers between devices, on_device(): lax.all_to_all(real_part, 'spatial', split_axis=1, concat_axis=0, tiled=T...  94.7 us
    dot_general x8, matrix products, block_product(): jnp.einsum('...bi,bio->...bo', values, weight, precision=FULL_PRECISION)  92.7 us
    all_to_all x1, waiting for transfers between devices, on_device(): lax.all_to_all(real_part, 'spatial', split_axis=0, concat_axis=1, tiled=T...  91.5 us
  transfers between devices with their start and end apart: 5, of which 5 were waited for; matrix products, arithmetic and copies ran while one was open for 2% of the time, Pallas kernels for 0%

profile of v1, /device:TPU:0, one launch (start us, length us, event | category | flops | bytes accessed | tf_op | source)
XLA Modules:
  0.0 2972.7 jit_solution(14970059498883837415)
XLA Ops:
  37.8 12.0 fusion.94
  56.2 95.7 %all-to-all-done.1 = f32[32,64,768]{2,0,1:T(8,128)} async-done(((f32[32,64,768]{2,0,1:T(8,128)}), f32[32,64,768]{2,0,1:T(8,128)}, u32[]{:S(2)}, u32[]{:S(2)}) %all-to-all-start.1) | async-done | bytes 6291488 | tf_op jit(solution)/shard_map/all_to_all | solution.py:142
  151.9 28.5 all-to-all-start
  199.8 94.7 %all-to-all-done = f32[32,64,768]{2,0,1:T(8,128)} async-done(((f32[32,64,768]{2,0,1:T(8,128)}), f32[32,64,768]{2,0,1:T(8,128)}, u32[]{:S(2)}, u32[]{:S(2)}) %all-to-all-start) | async-done | bytes 6291488 | tf_op jit(solution)/shard_map/all_to_all | solution.py:141
  308.7 9.9 reshape.102
  318.7 13.7 fusion.58
  332.4 9.9 fusion.60
  350.4 9.9 reshape.101
  360.3 13.1 add_maximum_fusion
  402.5 14.9 select_bitcast_fusion
  417.4 10.9 copy.70
  438.0 12.2 select_bitcast_fusion.1
  450.3 11.0 copy.69
  495.0 28.3 all-to-all-start.2
  545.7 91.5 %all-to-all-done.2 = f32[512,4,768]{2,1,0:T(4,128)} async-done(((f32[512,4,768]{2,1,0:T(4,128)}), f32[512,4,768]{2,1,0:T(4,128)}, u32[]{:S(2)}, u32[]{:S(2)}) %all-to-all-start.2) | async-done | bytes 6291488 | tf_op jit(solution)/shard_map/all_to_all | solution.py:148
  637.3 28.1 all-to-all-start.3
  684.3 95.2 %all-to-all-done.3 = f32[512,4,768]{2,1,0:T(4,128)} async-done(((f32[512,4,768]{2,1,0:T(4,128)}), f32[512,4,768]{2,1,0:T(4,128)}, u32[]{:S(2)}, u32[]{:S(2)}) %all-to-all-start.3) | async-done | bytes 6291488 | tf_op jit(solution)/shard_map/all_to_all | solution.py:149
  798.0 15.2 fusion.134
  813.1 19.3 fusion.262
  837.0 126.3 %fusion.2.clone.6 = bf16[4096,3072]{1,0:T(8,128)(2,1)} fusion(bf16[4096,768]{1,0:T(8,128)(2,1)S(1)} %fusion.47, bf16[768,3072]{1,0:T(8,128)(2,1)} %param.23, f32[3072]{0:T(1024)S(1)} %copy-done.22), kind=kOutput, calls=%fused_computation.3.clone.clone.clone.clone.clone.1 | convolution fusion | flops 20157825024 | bytes 36188160 | tf_op jit(solution)/shard_map/dot_general | solution.py:155
  963.3 26.5 fusion.49
  998.7 1919.6 %all-gather.3.cloned.1.call-done = f32[256,128,768]{2,1,0:T(8,128)} async-done(((f32[32,128,768]{2,1,0:T(8,128)}), f32[256,128,768]{2,1,0:T(8,128)}) %all-gather.3.cloned.1.call-update) | async-done | bytes 100663312 | tf_op jit(solution)/shard_map/all_gather | solution.py:165
  2918.3 36.0 %reduce_sum.49 = f32[32,128,768]{2,1,0:T(8,128)} reduce(f32[8,32,128,768]{3,2,1,0:T(8,128)} %bitcast.61, f32[]{:T(128)} %constant.29.clone.1), dimensions={0}, to_apply=%region_4.6 | reduce | flops 22020096 | bytes 113246208 | tf_op jit(solution)/shard_map/reduce_sum | solution.py:165
  2954.3 11.2 subtract_convert_fusion
  (121 shorter events, 224.1 us)
Async XLA Ops:
  11.8 26.0 copy-start.10
  14.2 23.6 copy-start.12
  30.3 121.5 %all-to-all-start.1 = ((f32[32,64,768]{2,0,1:T(8,128)}), f32[32,64,768]{2,0,1:T(8,128)}, u32[]{:S(2)}, u32[]{:S(2)}) async-start(f32[32,64,768]{2,0,1:T(8,128)} %copy.60), calls=%async_computation.1 | async-start | bytes 12582912 | tf_op jit(solution)/shard_map/all_to_all | solution.py:142
  56.2 124.2 %copy-start.14 = (f32[2,8,96]{2,1,0:T(8,128)S(1)}, f32[2,8,96]{2,1,0:T(8,128)}, u32[]{:S(2)}) copy-start(f32[2,8,96]{2,1,0:T(8,128)} %param.18) | copy-start | bytes 18436
  56.2 124.3 %copy-start.15 = (f32[2,8,96]{2,1,0:T(8,128)S(1)}, f32[2,8,96]{2,1,0:T(8,128)}, u32[]{:S(2)}) copy-start(f32[2,8,96]{2,1,0:T(8,128)} %param.20) | copy-start | bytes 18436
  151.9 142.6 %all-to-all-start = ((f32[32,64,768]{2,0,1:T(8,128)}), f32[32,64,768]{2,0,1:T(8,128)}, u32[]{:S(2)}, u32[]{:S(2)}) async-start(f32[32,64,768]{2,0,1:T(8,128)} %copy.57), calls=%async_computation | async-start | bytes 12582912 | tf_op jit(solution)/shard_map/all_to_all | solution.py:141
  199.8 101.1 %slice-start.10 = ((s8[6291456]{0:T(1024)(128)(4,1)}), s8[2097152]{0:T(1024)(128)(4,1)S(1)}, s32[]{:S(2)}) async-start(s8[6291456]{0:T(1024)(128)(4,1)} %bitcast.201), calls=%async_computation.15 | async-start | bytes 4194304
  308.7 9.9 copy-start.6
  318.6 13.7 copy-start.1
  318.6 23.6 slice-start.4
  318.7 23.6 slice-start.8
  360.3 13.2 copy-start.7
  373.5 19.4 slice-start
  373.5 19.4 slice-start.6
  402.5 14.9 copy-start.2
  494.9 36.9 %slice-start.2 = ((s8[6291456]{0:T(1024)(128)(4,1)}), s8[2097152]{0:T(1024)(128)(4,1)S(1)}, s32[]{:S(2)}) async-start(s8[6291456]{0:T(1024)(128)(4,1)} %bitcast.185), calls=%async_computation.7 | async-start | bytes 4194304
  495.0 142.3 %all-to-all-start.2 = ((f32[512,4,768]{2,1,0:T(4,128)}), f32[512,4,768]{2,1,0:T(4,128)}, u32[]{:S(2)}, u32[]{:S(2)}) async-start(f32[512,4,768]{2,1,0:T(4,128)} %copy.72), calls=%async_computation.2 | async-start | bytes 12582912 | tf_op jit(solution)/shard_map/all_to_all | solution.py:148
  637.3 142.2 %all-to-all-start.3 = ((f32[512,4,768]{2,1,0:T(4,128)}), f32[512,4,768]{2,1,0:T(4,128)}, u32[]{:S(2)}, u32[]{:S(2)}) async-start(f32[512,4,768]{2,1,0:T(4,128)} %copy.76), calls=%async_computation.3 | async-start | bytes 12582912 | tf_op jit(solution)/shard_map/all_to_all | solution.py:149
  665.4 2252.9 %all-gather.3.cloned.1.call-start = ((), (), s32[]{:S(2)}) async-start(), calls=%async_computation.4 | async-start | bytes 113246208 | tf_op jit(solution)/shard_map/all_gather | solution.py:165
  797.9 15.2 copy-start.11
  797.9 15.2 copy-start.13
  798.0 15.2 copy-start.17
  798.0 15.2 copy-start.19
  837.0 126.3 %copy-start.23 = (f32[768]{0:T(1024)S(1)}, f32[768]{0:T(1024)}, u32[]{:S(2)}) copy-start(f32[768]{0:T(1024)} %param.26) | copy-start | bytes 9220
  (17 other events, 108.4 us)
Sparse Core Ops, SparseCore 0:
  998.8 1919.4 all-gather.2
